TPU v7x, 32 devices: a whole 2x2x4 slice. The times are simulated.
32 devices in a mesh: mem: 8 (over z, y), job: 4 (over x, core).
Axes of the slice: x: 2, y: 2, z: 4, core: 2. Of those that a mesh axis runs over, the one named last changes fastest.
Arguments:
- pair_cost: bfloat16 [1536, 128, 128], P(('mem', 'job')), may hold values from -6 to 6
- pair_coef: bfloat16 [1536, 128, 128], P(('mem', 'job')), may hold values from 0.049804688 to 0.5
- slot_member: int32 [32, 48], P(('mem', 'job')), may hold values from 0 to 31, never falling along the last dimension, each value on 1 to 4 neighbouring positions
- slot_owner: int32 [32, 48, 1], P(('mem', 'job')), may hold values from 0 to 7; in each aligned block of 48 rows (0 to 47, 48 to 95, ..., all dimensions but the last counted through in order) at most 9 rows name the same one
- slot_local: int32 [32, 48], P(('mem', 'job')), may hold values from 0 to 15
- duals: float32 [512, 128], P(('mem', 'job')), may hold values from 0.1 to 3
- capacity: int32 [512, 128], P(('mem', 'job')), may hold values from 0 to 39
Outputs:
- primal: bfloat16 [1536, 128, 128], P(('mem', 'job'))
- gradient: float32 [512, 128], P(('mem', 'job'))
- member_share: float32 [256, 128], P('mem')
Inputs may be any that keep to these rules, and one draw needn't show every extreme that they name: `slot_member`: in each device's row the values never fall, every value appears, none more than 4 times, and one exactly 4 times. `slot_owner`: among the 48 entries of one device no value appears more than 9 times, and in some devices one appears exactly 9 times.
All inputs are finite; a program needn't handle non-finite values.
Results may differ from a plain program's by a relative error of at most 0.001.
Values sent between devices are 32-bit elements; how exact they have to be, the bound alone decides.
A program may use at most 64 MiB of HBM per device.

v0:
```python
import jax
import jax.numpy as jnp
from jax import lax
from jax.sharding import PartitionSpec as P

MB_DEV = 32
RIDGE = 1.0


def allocate(pair_cost, pair_coef, dual_rows):
    reduced = pair_cost.astype(jnp.float32) + pair_coef.astype(jnp.float32) * dual_rows[:, None, :]
    allocation = jnp.clip(-reduced / RIDGE, 0.0, 1.0)
    column_part = jnp.sum(pair_coef.astype(jnp.float32) * allocation, axis=1)
    row_part = jnp.sum(allocation, axis=2)
    return (allocation.astype(jnp.bfloat16), column_part, row_part)


def per_device(pair_cost, pair_coef, slot_member, slot_owner, slot_local, duals, capacity):
    slot_count = pair_cost.shape[0]
    block_size = pair_cost.shape[1]
    job_blocks = duals.shape[0]
    mem_count = lax.axis_size("mem")
    owner_index = slot_owner[0, :, 0]
    local_index = slot_local[0]
    peer_slots = max(2, (3 * slot_count + 2 * mem_count - 1) // (2 * mem_count))
    owner_table = (owner_index[:, None] == jnp.arange(mem_count, dtype=jnp.int32)[None, :]).astype(
        jnp.int32
    )
    slot_rank = jnp.sum((jnp.cumsum(owner_table, axis=0) - owner_table) * owner_table, axis=1)
    position = owner_index * peer_slots + slot_rank
    requests = jnp.zeros((mem_count * peer_slots,), jnp.int32).at[position].set(local_index)
    requests = requests.reshape(mem_count, peer_slots)
    received = lax.all_to_all(requests, "mem", split_axis=0, concat_axis=0, tiled=True)
    replies = duals[received]
    fetched, received = (
        lax.all_to_all(replies, "mem", split_axis=0, concat_axis=0, tiled=True),
        received,
    )
    dual_rows = fetched.reshape(mem_count * peer_slots, block_size)[position]
    primal, column_part, row_part = allocate(pair_cost, pair_coef, dual_rows)
    outgoing = (
        jnp.zeros((mem_count * peer_slots, block_size), jnp.float32).at[position].set(column_part)
    )
    incoming = lax.all_to_all(
        outgoing.reshape(mem_count, peer_slots, block_size),
        "mem",
        split_axis=0,
        concat_axis=0,
        tiled=True,
    )
    totals = jax.ops.segment_sum(
        incoming.reshape(mem_count * peer_slots, block_size),
        received.reshape(-1),
        num_segments=job_blocks,
    )
    gradient = totals - capacity.astype(jnp.float32)
    member_table = (jnp.arange(MB_DEV, dtype=jnp.int32)[:, None] == slot_member[0][None, :]).astype(
        jnp.float32
    )
    member_part = jnp.dot(
        member_table, row_part, precision=lax.Precision.HIGHEST, preferred_element_type=jnp.float32
    )
    member_share = lax.psum(member_part, "job") / block_size
    return (primal, gradient, member_share)


def solution(mesh):
    placed = (
        P(("mem", "job"), None, None),
        P(("mem", "job"), None, None),
        P(("mem", "job"), None),
        P(("mem", "job"), None, None),
        P(("mem", "job"), None),
        P(("mem", "job"), None),
        P(("mem", "job"), None),
    )
    return jax.shard_map(
        per_device,
        mesh=mesh,
        in_specs=placed,
        out_specs=(P(("mem", "job"), None, None), P(("mem", "job"), None), P("mem", None)),
        check_vma=False,
    )
```

profile of v0, /device:TPU:0, one launch (start us, length us, event | category | flops | bytes accessed | tf_op | source)
XLA Modules:
  0.0 57.0 jit_solution(11159333356886695551)
XLA Ops:
  0.6 0.0 copy-start
  0.6 0.7 %fusion.6 = s32[48,8]{1,0:T(8,128)S(1)} fusion(s32[48]{0:T(128)} %bitcast.20), kind=kLoop, calls=%fused_computation.15 | loop fusion | flops 768 | bytes 1728 | tf_op jit(solution)/shard_map/convert_element_type | solution.py:26
  1.4 0.1 reduce_window_sum.11
  1.5 0.8 %select_reduce_fusion = s32[48]{0:T(128)S(1)} fusion(s32[48,8]{1,0:T(8,128)S(1)} %reduce_window_sum.11, s32[48]{0:T(128)} %bitcast.21), kind=kLoop, calls=%fused_computation.13 | loop fusion | flops 1872 | bytes 1920 | tf_op jit(solution)/shard_map/reduce_sum | solution.py:29
  2.3 0.7 %fusion.13 = s32[48]{0:T(128)S(1)} fusion(s32[48]{0:T(128)S(1)} %select_reduce_fusion, s32[1,48,1]{1,2,0:T(1,128)} %param.10), kind=kLoop, calls=%fused_computation.29 | loop fusion | flops 240 | bytes 576 | tf_op jit(solution)/shard_map/select_n | solution.py:31
  3.0 0.9 %scatter_custom_fusion = s32[72]{0:T(128)S(1)} fusion(s32[48]{0:T(128)S(1)} %fusion.13, s32[48]{0:T(128)} %bitcast.23, s32[]{:T(128)} %constant.8.clone.1), kind=kCustom, calls=%fused_computation.31 | custom fusion | bytes 800 | tf_op jit(solution)/shard_map/scatter | solution.py:31
  3.8 0.1 all_to_all.14
  3.9 13.6 %all_to_all.22 = s32[8,1,9]{2,1,0:T(1,128)S(1)} all-to-all(s32[8,1,9]{2,1,0:T(1,128)S(1)} %bitcast.19), channel_id=1, replica_groups=mesh['mem'=8,'job'=4] {'mem'}, dimensions={0} | all-to-all | bytes 576 | tf_op jit(solution)/shard_map/all_to_all | solution.py:33
  17.5 0.1 reshape.83
  17.6 0.0 copy-done
  17.6 0.6 %gather_fusion = f32[72,128]{1,0:T(8,128)S(1)} fusion(f32[16,128]{1,0:T(8,128)S(1)} %copy-done, s32[1024]{0:T(1024)S(1)} %pad_clamp_fusion.1), kind=kCustom, calls=%fused_computation | custom fusion | bytes 74016 | tf_op jit(solution)/shard_map/gather | solution.py:34
  18.2 0.6 %reshape.82 = f32[8,9,128]{2,1,0:T(8,128)} reshape(f32[72,128]{1,0:T(8,128)S(1)} %gather_fusion) | data formatting | bytes 73728 | tf_op jit(solution)/shard_map/gather | solution.py:34
  18.8 3.4 %all-to-all-start.1 = ((f32[8,9,128]{2,1,0:T(8,128)}), f32[8,9,128]{2,1,0:T(8,128)S(1)}, u32[]{:S(2)}, u32[]{:S(2)}) async-start(f32[8,9,128]{2,1,0:T(8,128)} %reshape.82), calls=%async_computation.1 | async-start | bytes 131072 | tf_op jit(solution)/shard_map/all_to_all | solution.py:36
  22.2 0.5 broadcast.65
  22.7 0.7 %reduce.3 = s32[8,9]{1,0:T(8,128)S(1)} reduce(s32[8,1,9]{2,1,0:T(1,128)S(1)} %all_to_all.22, s32[]{:T(128)} %broadcast.65), dimensions={1}, to_apply=%all_to_all.15.reduce_sub_computation.3 | reduce | bytes 580 | tf_op jit(solution)/shard_map/all_to_all | solution.py:33
  23.4 0.1 reshape.115
  23.5 5.6 %all-to-all-done.1 = f32[8,9,128]{2,1,0:T(8,128)S(1)} async-done(((f32[8,9,128]{2,1,0:T(8,128)}), f32[8,9,128]{2,1,0:T(8,128)S(1)}, u32[]{:S(2)}, u32[]{:S(2)}) %all-to-all-start.1) | async-done | bytes 36896 | tf_op jit(solution)/shard_map/all_to_all | solution.py:36
  29.0 0.6 %gather_fusion.1 = f32[48,128]{1,0:T(8,128)S(1)} fusion(f32[72,128]{1,0:T(8,128)S(1)} %reshape.78, s32[1024]{0:T(1024)S(1)} %pad_clamp_fusion), kind=kCustom, calls=%fused_computation.1 | custom fusion | bytes 49344 | tf_op jit(solution)/shard_map/gather | solution.py:39
  29.6 0.0 copy-start.2
  29.6 0.0 copy-start.1
  29.6 4.1 %fusion.4 = (f32[48,128]{1,0:T(8,128)S(1)}, f32[48,128]{1,0:T(8,128)S(1)}, bf16[48,128,128]{2,1,0:T(8,128)(2,1)}) fusion(bf16[48,128,128]{2,1,0:T(8,128)(2,1)} %param.8, bf16[48,128,128]{2,1,0:T(8,128)(2,1)} %param.7, f32[48,128]{1,0:T(8,128)S(1)} %gather_fusion.1), kind=kLoop, calls=%fused_computation.11 | loop fusion | flops 7852032 | bytes 4792320 | tf_op jit(solution)/shard_map/reduce_sum | solution.py:14
  33.8 0.0 copy-done.2
  33.8 0.1 fusion.9
  33.9 10.1 %psum.7 = f32[32,128]{1,0:T(8,128)S(1)} all-reduce(f32[32,128]{1,0:T(8,128)S(1)} %fusion.9), channel_id=1, replica_groups=mesh['mem'=8,'job'=4] {'job'}, use_global_device_ids=true, to_apply=%region_7.8 | all-reduce | flops 4096 | bytes 32768 | tf_op jit(solution)/shard_map/psum | solution.py:63
  44.0 0.7 %scatter_custom_fusion.1 = f32[72,128]{1,0:T(8,128)S(1)} fusion(s32[48]{0:T(128)S(1)} %fusion.13, f32[48,128]{1,0:T(8,128)S(1)} %get-tuple-element.4, f32[]{:T(128)} %constant.7.clone.1), kind=kCustom, calls=%fused_computation.16 | custom fusion | bytes 36868 | tf_op jit(solution)/shard_map/scatter | solution.py:42
  44.7 0.6 %reshape.79 = f32[8,9,128]{2,1,0:T(8,128)} reshape(f32[72,128]{1,0:T(8,128)S(1)} %scatter_custom_fusion.1) | data formatting | bytes 73728 | tf_op jit(solution)/shard_map/reshape | solution.py:45
  45.3 3.3 %all-to-all-start.2 = ((f32[8,9,128]{2,1,0:T(8,128)}), f32[8,9,128]{2,1,0:T(8,128)S(1)}, u32[]{:S(2)}, u32[]{:S(2)}) async-start(f32[8,9,128]{2,1,0:T(8,128)} %reshape.79), calls=%async_computation.2 | async-start | bytes 131072 | tf_op jit(solution)/shard_map/all_to_all | solution.py:44
  48.7 0.6 %broadcast_multiply_fusion = f32[32,128]{1,0:T(8,128)} fusion(f32[32,128]{1,0:T(8,128)S(1)} %psum.7), kind=kLoop, calls=%fused_computation.21 | loop fusion | flops 4096 | bytes 32768 | tf_op jit(solution)/shard_map/div | solution.py:63
  49.3 6.2 %all-to-all-done.2 = f32[8,9,128]{2,1,0:T(8,128)S(1)} async-done(((f32[8,9,128]{2,1,0:T(8,128)}), f32[8,9,128]{2,1,0:T(8,128)S(1)}, u32[]{:S(2)}, u32[]{:S(2)}) %all-to-all-start.2) | async-done | bytes 36896 | tf_op jit(solution)/shard_map/all_to_all | solution.py:44
  55.5 0.8 %scatter_custom_fusion.2 = f32[16,128]{1,0:T(8,128)S(1)} fusion(s32[72]{0:T(128)S(1)} %reshape.115, f32[72,128]{1,0:T(8,128)S(1)} %reshape.117, f32[]{:T(128)} %constant.7.clone.1), kind=kCustom, calls=%fused_computation.26 | custom fusion | flops 9216 | bytes 8196 | tf_op jit(solution)/shard_map/scatter-add | solution.py:51
  56.3 0.0 copy-done.1
  56.3 0.6 %convert_subtract_fusion = f32[16,128]{1,0:T(8,128)} fusion(f32[16,128]{1,0:T(8,128)S(1)} %scatter_custom_fusion.2, s32[16,128]{1,0:T(8,128)S(1)} %copy-done.1), kind=kLoop, calls=%fused_computation.23 | loop fusion | flops 4096 | bytes 24576 | tf_op jit(solution)/shard_map/sub | solution.py:56
  (5 shorter events, 0.0 us)
Async XLA Ops:
  0.6 17.0 %copy-start = (f32[16,128]{1,0:T(8,128)S(1)}, f32[16,128]{1,0:T(8,128)}, u32[]{:S(2)}) copy-start(f32[16,128]{1,0:T(8,128)} %param.12) | copy-start | bytes 24580
  18.8 10.2 %all-to-all-start.1 = ((f32[8,9,128]{2,1,0:T(8,128)}), f32[8,9,128]{2,1,0:T(8,128)S(1)}, u32[]{:S(2)}, u32[]{:S(2)}) async-start(f32[8,9,128]{2,1,0:T(8,128)} %reshape.82), calls=%async_computation.1 | async-start | bytes 131072 | tf_op jit(solution)/shard_map/all_to_all | solution.py:36
  29.6 4.1 %copy-start.2 = (s32[1,48]{1,0:T(1,128)S(1)}, s32[1,48]{1,0:T(1,128)}, u32[]{:S(2)}) copy-start(s32[1,48]{1,0:T(1,128)} %param.9) | copy-start | bytes 580
  29.6 26.7 %copy-start.1 = (s32[16,128]{1,0:T(8,128)S(1)}, s32[16,128]{1,0:T(8,128)}, u32[]{:S(2)}) copy-start(s32[16,128]{1,0:T(8,128)} %param.13) | copy-start | bytes 24580
  45.3 10.2 %all-to-all-start.2 = ((f32[8,9,128]{2,1,0:T(8,128)}), f32[8,9,128]{2,1,0:T(8,128)S(1)}, u32[]{:S(2)}, u32[]{:S(2)}) async-start(f32[8,9,128]{2,1,0:T(8,128)} %reshape.79), calls=%async_computation.2 | async-start | bytes 131072 | tf_op jit(solution)/shard_map/all_to_all | solution.py:44
where the time goes:
time: 57.4 us; the launch traced here: 57 us
  blocking collectives  23.7 us (41%)
  waiting for transfers between devices  11.8 us (21%)
  other arithmetic  9.12 us (16%)
  starting transfers between devices  6.7 us (12%)
  local copies, waits for them, and re-layouts  4.76 us (8%)
  between operations  0.73 us (1%)
    all_to_all x1, blocking collectives, per_device(): lax.all_to_all(requests, 'mem', split_axis=0, concat_axis=0, tiled=True)  13.6 us
    psum x1, blocking collectives, per_device(): member_share = lax.psum(member_part, 'job') / block_size  10.1 us
    all_to_all x1, waiting for transfers between devices, per_device(): lax.all_to_all(outgoing.reshape(mem_count, peer_slots, block_size), 'mem'...  6.23 us
    all_to_all x1, waiting for transfers between devices, per_device(): lax.all_to_all(replies, 'mem', split_axis=0, concat_axis=0, tiled=True)  5.57 us
    reduce_sum x1, other arithmetic, allocate(): row_part = jnp.sum(allocation, axis=2)  4.11 us
    all_to_all x1, starting transfers between devices, per_device(): lax.all_to_all(replies, 'mem', split_axis=0, concat_axis=0, tiled=True)  3.35 us
    all_to_all x1, starting transfers between devices, per_device(): lax.all_to_all(outgoing.reshape(mem_count, peer_slots, block_size), 'mem'...  3.35 us
    gather x2, local copies, waits for them, and re-layouts, per_device(): replies = duals[received]  1.24 us
  transfers between devices with their start and end apart: 2, of which 2 were waited for; matrix products, arithmetic and copies ran while one was open for 3% of the time, Pallas kernels for 0%

commit v1 on v0

--- a/solution.py
+++ b/solution.py
@@ -30,7 +30,19 @@
     position = owner_index * peer_slots + slot_rank
     requests = jnp.zeros((mem_count * peer_slots,), jnp.int32).at[position].set(local_index)
     requests = requests.reshape(mem_count, peer_slots)
-    received = lax.all_to_all(requests, "mem", split_axis=0, concat_axis=0, tiled=True)
+    ways, here = (lax.axis_size("mem"), lax.axis_index("mem"))
+    width = requests.shape[0] // ways
+    shape = list(requests.shape)
+    shape[0] = width
+    height = shape[0]
+    shape[0] = height * ways
+    full = jnp.zeros(shape, requests.dtype)
+    for mask in range(ways):
+        part = lax.dynamic_slice_in_dim(requests, (here ^ mask) * width, width, axis=0)
+        if mask:
+            part = lax.ppermute(part, "mem", [(d, d ^ mask) for d in range(ways)])
+        full = lax.dynamic_update_slice_in_dim(full, part, (here ^ mask) * height, axis=0)
+    received = full
     replies = duals[received]
     fetched, received = (
         lax.all_to_all(replies, "mem", split_axis=0, concat_axis=0, tiled=True),

time: 57.4 us -> 67.3 us (1.17)
  starting transfers between devices: 6.7 us -> 23.6 us
  blocking collectives: 23.7 us -> 10.1 us
  waiting for transfers between devices: 11.8 us -> 19.3 us
    ppermute x0 -> x7, starting transfers between devices: none -> 14.4 us  [per_device(): part = lax.ppermute(part, 'mem', [(d, d ^ mask) for d in range(ways)])]
    all_to_all x1 -> x0, blocking collectives: 13.6 us -> none  [per_device(): lax.all_to_all(requests, 'mem', split_axis=0, concat_axis=0, tiled=True)]
    ppermute x0 -> x7, waiting for transfers between devices: none -> 6.25 us  [per_device(): part = lax.ppermute(part, 'mem', [(d, d ^ mask) for d in range(ways)])]
    all_to_all x1, starting transfers between devices: 3.35 us -> 5.92 us  [per_device(): lax.all_to_all(replies, 'mem', split_axis=0, concat_axis=0, tiled=True)]
    all_to_all x1, waiting for transfers between devices: 5.57 us -> 6.82 us  [per_device(): lax.all_to_all(replies, 'mem', split_axis=0, concat_axis=0, tiled=True)]
  transfers between devices with their start and end apart: 2 -> 9, of which waited for: 2 -> 5; matrix products, arithmetic and copies ran while one was open for 3% -> 1% of each run, Pallas kernels for 0% -> 0%
where the time goes in v1:
time: 67.3 us; the launch traced here: 67 us
  starting transfers between devices  23.6 us (35%)
  waiting for transfers between devices  19.3 us (29%)
  blocking collectives  10.1 us (15%)
  other arithmetic  8.46 us (13%)
  local copies, waits for them, and re-layouts  4.52 us (7%)
  between operations  0.79 us (1%)
    ppermute x7, starting transfers between devices, per_device(): part = lax.ppermute(part, 'mem', [(d, d ^ mask) for d in range(ways)])  14.4 us
    psum x1, blocking collectives, per_device(): member_share = lax.psum(member_part, 'job') / block_size  10.1 us
    all_to_all x1, waiting for transfers between devices, per_device(): lax.all_to_all(replies, 'mem', split_axis=0, concat_axis=0, tiled=True)  6.82 us
    ppermute x7, waiting for transfers between devices, per_device(): part = lax.ppermute(part, 'mem', [(d, d ^ mask) for d in range(ways)])  6.25 us
    all_to_all x1, waiting for transfers between devices, per_device(): lax.all_to_all(outgoing.reshape(mem_count, peer_slots, block_size), 'mem'...  6.23 us
    all_to_all x1, starting transfers between devices, per_device(): lax.all_to_all(replies, 'mem', split_axis=0, concat_axis=0, tiled=True)  5.92 us
    reduce_sum x1, other arithmetic, allocate(): row_part = jnp.sum(allocation, axis=2)  4.11 us
    all_to_all x1, starting transfers between devices, per_device(): lax.all_to_all(outgoing.reshape(mem_count, peer_slots, block_size), 'mem'...  3.35 us
  transfers between devices with their start and end apart: 9, of which 5 were waited for; matrix products, arithmetic and copies ran while one was open for 1% of the time, Pallas kernels for 0%

profile of v1, /device:TPU:0, one launch (start us, length us, event | category | flops | bytes accessed | tf_op | source)
XLA Modules:
  0.0 67.0 jit_solution(12992384645191144618)
XLA Ops:
  0.7 0.7 %fusion.6 = s32[48,8]{1,0:T(8,128)S(1)} fusion(s32[48]{0:T(128)} %bitcast.14), kind=kLoop, calls=%fused_computation.15 | loop fusion | flops 768 | bytes 1728 | tf_op jit(solution)/shard_map/convert_element_type | solution.py:26
  1.5 0.8 %select_reduce_fusion = s32[48]{0:T(128)S(1)} fusion(s32[48,8]{1,0:T(8,128)S(1)} %reduce_window_sum.11, s32[48]{0:T(128)} %bitcast.15), kind=kLoop, calls=%fused_computation.13 | loop fusion | flops 1872 | bytes 1920 | tf_op jit(solution)/shard_map/reduce_sum | solution.py:29
  2.3 0.7 fusion.13
  3.0 0.9 %scatter_custom_fusion = s32[72]{0:T(128)S(1)} fusion(s32[48]{0:T(128)S(1)} %fusion.13, s32[48]{0:T(128)} %bitcast.17, s32[]{:T(128)} %constant.18.clone.1), kind=kCustom, calls=%fused_computation.39 | custom fusion | bytes 800 | tf_op jit(solution)/shard_map/scatter | solution.py:31
  3.8 0.1 reshape.48
  4.0 6.1 %collective-permute-start.6 = (s32[1,9]{1,0:T(1,128)S(1)}, s32[1,9]{1,0:T(1,128)S(1)}, u32[]{:S(2)}, u32[]{:S(2)}) collective-permute-start(s32[1,9]{1,0:T(1,128)S(1)} %get-tuple-element.6), channel_id=1, source_target_pairs={{0,28},{4,24},{8,20},{12,16},{16,12},{20,8},{24,4},{28,0},{1,29},{... | collective-permute-start | bytes 116 | tf_op jit(solution)/shard_map/ppermute | solution.py:43
  10.0 0.2 collective-permute-start.5
  10.3 0.7 %collective-permute-start.4 = (s32[1,9]{1,0:T(1,128)S(1)}, s32[1,9]{1,0:T(1,128)S(1)}, u32[]{:S(2)}, u32[]{:S(2)}) collective-permute-start(s32[1,9]{1,0:T(1,128)S(1)} %get-tuple-element.8), channel_id=1, source_target_pairs={{0,20},{4,16},{8,28},{12,24},{16,4},{20,0},{24,12},{28,8},{1,21},{... | collective-permute-start | bytes 116 | tf_op jit(solution)/shard_map/ppermute | solution.py:43
  11.0 2.0 %collective-permute-start.3 = (s32[1,9]{1,0:T(1,128)S(1)}, s32[1,9]{1,0:T(1,128)S(1)}, u32[]{:S(2)}, u32[]{:S(2)}) collective-permute-start(s32[1,9]{1,0:T(1,128)S(1)} %get-tuple-element.9), channel_id=1, source_target_pairs={{0,16},{4,20},{8,24},{12,28},{16,0},{20,4},{24,8},{28,12},{1,17},{... | collective-permute-start | bytes 116 | tf_op jit(solution)/shard_map/ppermute | solution.py:43
  13.1 1.6 %collective-permute-start = (s32[1,9]{1,0:T(1,128)S(1)}, s32[1,9]{1,0:T(1,128)S(1)}, u32[]{:S(2)}, u32[]{:S(2)}) collective-permute-start(s32[1,9]{1,0:T(1,128)S(1)} %get-tuple-element.12), channel_id=1, source_target_pairs={{0,4},{4,0},{8,12},{12,8},{16,20},{20,16},{24,28},{28,24},{1,5},{5... | collective-permute-start | bytes 116 | tf_op jit(solution)/shard_map/ppermute | solution.py:43
  14.7 1.9 %collective-permute-done = s32[1,9]{1,0:T(1,128)S(1)} collective-permute-done((s32[1,9]{1,0:T(1,128)S(1)}, s32[1,9]{1,0:T(1,128)S(1)}, u32[]{:S(2)}, u32[]{:S(2)}) %collective-permute-start) | collective-permute-done | bytes 68 | tf_op jit(solution)/shard_map/ppermute | solution.py:43
  16.6 1.4 %collective-permute-start.1 = (s32[1,9]{1,0:T(1,128)S(1)}, s32[1,9]{1,0:T(1,128)S(1)}, u32[]{:S(2)}, u32[]{:S(2)}) collective-permute-start(s32[1,9]{1,0:T(1,128)S(1)} %get-tuple-element.11), channel_id=1, source_target_pairs={{0,8},{4,12},{8,0},{12,4},{16,24},{20,28},{24,16},{28,20},{1,9},{5... | collective-permute-start | bytes 116 | tf_op jit(solution)/shard_map/ppermute | solution.py:43
  18.0 2.2 %collective-permute-done.1 = s32[1,9]{1,0:T(1,128)S(1)} collective-permute-done((s32[1,9]{1,0:T(1,128)S(1)}, s32[1,9]{1,0:T(1,128)S(1)}, u32[]{:S(2)}, u32[]{:S(2)}) %collective-permute-start.1) | collective-permute-done | bytes 68 | tf_op jit(solution)/shard_map/ppermute | solution.py:43
  20.2 2.3 %collective-permute-start.2 = (s32[1,9]{1,0:T(1,128)S(1)}, s32[1,9]{1,0:T(1,128)S(1)}, u32[]{:S(2)}, u32[]{:S(2)}) collective-permute-start(s32[1,9]{1,0:T(1,128)S(1)} %get-tuple-element.10), channel_id=1, source_target_pairs={{0,12},{4,8},{8,4},{12,0},{16,28},{20,24},{24,20},{28,16},{1,13},{... | collective-permute-start | bytes 116 | tf_op jit(solution)/shard_map/ppermute | solution.py:43
  22.5 2.2 %collective-permute-done.2 = s32[1,9]{1,0:T(1,128)S(1)} collective-permute-done((s32[1,9]{1,0:T(1,128)S(1)}, s32[1,9]{1,0:T(1,128)S(1)}, u32[]{:S(2)}, u32[]{:S(2)}) %collective-permute-start.2) | collective-permute-done | bytes 68 | tf_op jit(solution)/shard_map/ppermute | solution.py:43
  24.9 0.1 reshape.54
  25.0 0.6 gather_fusion
  25.6 0.6 reshape.53
  26.2 5.9 %all-to-all-start = ((f32[8,9,128]{2,1,0:T(8,128)}), f32[8,9,128]{2,1,0:T(8,128)S(1)}, u32[]{:S(2)}, u32[]{:S(2)}) async-start(f32[8,9,128]{2,1,0:T(8,128)} %reshape.53), calls=%async_computation | async-start | bytes 131072 | tf_op jit(solution)/shard_map/all_to_all | solution.py:48
  32.1 0.1 reshape.86
  32.2 6.8 %all-to-all-done = f32[8,9,128]{2,1,0:T(8,128)S(1)} async-done(((f32[8,9,128]{2,1,0:T(8,128)}), f32[8,9,128]{2,1,0:T(8,128)S(1)}, u32[]{:S(2)}, u32[]{:S(2)}) %all-to-all-start) | async-done | bytes 36896 | tf_op jit(solution)/shard_map/all_to_all | solution.py:48
  39.0 0.6 gather_fusion.1
  39.6 4.1 %fusion.4 = (f32[48,128]{1,0:T(8,128)S(1)}, f32[48,128]{1,0:T(8,128)S(1)}, bf16[48,128,128]{2,1,0:T(8,128)(2,1)}) fusion(bf16[48,128,128]{2,1,0:T(8,128)(2,1)} %param.8, bf16[48,128,128]{2,1,0:T(8,128)(2,1)} %param.7, f32[48,128]{1,0:T(8,128)S(1)} %gather_fusion.1), kind=kLoop, calls=%fused_computation.11 | loop fusion | flops 7852032 | bytes 4792320 | tf_op jit(solution)/shard_map/reduce_sum | solution.py:14
  43.8 0.1 fusion.9
  43.9 10.1 %psum.7 = f32[32,128]{1,0:T(8,128)S(1)} all-reduce(f32[32,128]{1,0:T(8,128)S(1)} %fusion.9), channel_id=1, replica_groups=mesh['mem'=8,'job'=4] {'job'}, use_global_device_ids=true, to_apply=%region_7.8 | all-reduce | flops 4096 | bytes 32768 | tf_op jit(solution)/shard_map/psum | solution.py:75
  54.0 0.7 %scatter_custom_fusion.1 = f32[72,128]{1,0:T(8,128)S(1)} fusion(s32[48]{0:T(128)S(1)} %fusion.13, f32[48,128]{1,0:T(8,128)S(1)} %get-tuple-element.4, f32[]{:T(128)} %constant.17.clone.1), kind=kCustom, calls=%fused_computation.16 | custom fusion | bytes 36868 | tf_op jit(solution)/shard_map/scatter | solution.py:54
  54.7 0.6 reshape.50
  55.3 3.3 %all-to-all-start.1 = ((f32[8,9,128]{2,1,0:T(8,128)}), f32[8,9,128]{2,1,0:T(8,128)S(1)}, u32[]{:S(2)}, u32[]{:S(2)}) async-start(f32[8,9,128]{2,1,0:T(8,128)} %reshape.50), calls=%async_computation.1 | async-start | bytes 131072 | tf_op jit(solution)/shard_map/all_to_all | solution.py:56
  58.7 0.6 broadcast_multiply_fusion
  59.3 6.2 %all-to-all-done.1 = f32[8,9,128]{2,1,0:T(8,128)S(1)} async-done(((f32[8,9,128]{2,1,0:T(8,128)}), f32[8,9,128]{2,1,0:T(8,128)S(1)}, u32[]{:S(2)}, u32[]{:S(2)}) %all-to-all-start.1) | async-done | bytes 36896 | tf_op jit(solution)/shard_map/all_to_all | solution.py:56
  65.5 0.8 %scatter_custom_fusion.2 = f32[16,128]{1,0:T(8,128)S(1)} fusion(s32[72]{0:T(128)S(1)} %reshape.86, f32[72,128]{1,0:T(8,128)S(1)} %reshape.88, f32[]{:T(128)} %constant.17.clone.1), kind=kCustom, calls=%fused_computation.26 | custom fusion | flops 9216 | bytes 8196 | tf_op jit(solution)/shard_map/scatter-add | solution.py:63
  66.4 0.6 convert_subtract_fusion
  (26 shorter events, 0.4 us)
Async XLA Ops:
  0.6 24.3 %copy-start = (f32[16,128]{1,0:T(8,128)S(1)}, f32[16,128]{1,0:T(8,128)}, u32[]{:S(2)}) copy-start(f32[16,128]{1,0:T(8,128)} %param.12) | copy-start | bytes 24580
  4.0 20.9 %collective-permute-start.6 = (s32[1,9]{1,0:T(1,128)S(1)}, s32[1,9]{1,0:T(1,128)S(1)}, u32[]{:S(2)}, u32[]{:S(2)}) collective-permute-start(s32[1,9]{1,0:T(1,128)S(1)} %get-tuple-element.6), channel_id=1, source_target_pairs={{0,28},{4,24},{8,20},{12,16},{16,12},{20,8},{24,4},{28,0},{1,29},{... | collective-permute-start | bytes 116 | tf_op jit(solution)/shard_map/ppermute | solution.py:43
  10.0 14.7 %collective-permute-start.5 = (s32[1,9]{1,0:T(1,128)S(1)}, s32[1,9]{1,0:T(1,128)S(1)}, u32[]{:S(2)}, u32[]{:S(2)}) collective-permute-start(s32[1,9]{1,0:T(1,128)S(1)} %get-tuple-element.7), channel_id=1, source_target_pairs={{0,24},{4,28},{8,16},{12,20},{16,8},{20,12},{24,0},{28,4},{1,25},{... | collective-permute-start | bytes 116 | tf_op jit(solution)/shard_map/ppermute | solution.py:43
  10.3 14.5 %collective-permute-start.4 = (s32[1,9]{1,0:T(1,128)S(1)}, s32[1,9]{1,0:T(1,128)S(1)}, u32[]{:S(2)}, u32[]{:S(2)}) collective-permute-start(s32[1,9]{1,0:T(1,128)S(1)} %get-tuple-element.8), channel_id=1, source_target_pairs={{0,20},{4,16},{8,28},{12,24},{16,4},{20,0},{24,12},{28,8},{1,21},{... | collective-permute-start | bytes 116 | tf_op jit(solution)/shard_map/ppermute | solution.py:43
  11.0 13.7 %collective-permute-start.3 = (s32[1,9]{1,0:T(1,128)S(1)}, s32[1,9]{1,0:T(1,128)S(1)}, u32[]{:S(2)}, u32[]{:S(2)}) collective-permute-start(s32[1,9]{1,0:T(1,128)S(1)} %get-tuple-element.9), channel_id=1, source_target_pairs={{0,16},{4,20},{8,24},{12,28},{16,0},{20,4},{24,8},{28,12},{1,17},{... | collective-permute-start | bytes 116 | tf_op jit(solution)/shard_map/ppermute | solution.py:43
  13.1 3.6 %collective-permute-start = (s32[1,9]{1,0:T(1,128)S(1)}, s32[1,9]{1,0:T(1,128)S(1)}, u32[]{:S(2)}, u32[]{:S(2)}) collective-permute-start(s32[1,9]{1,0:T(1,128)S(1)} %get-tuple-element.12), channel_id=1, source_target_pairs={{0,4},{4,0},{8,12},{12,8},{16,20},{20,16},{24,28},{28,24},{1,5},{5... | collective-permute-start | bytes 116 | tf_op jit(solution)/shard_map/ppermute | solution.py:43
  16.6 3.6 %collective-permute-start.1 = (s32[1,9]{1,0:T(1,128)S(1)}, s32[1,9]{1,0:T(1,128)S(1)}, u32[]{:S(2)}, u32[]{:S(2)}) collective-permute-start(s32[1,9]{1,0:T(1,128)S(1)} %get-tuple-element.11), channel_id=1, source_target_pairs={{0,8},{4,12},{8,0},{12,4},{16,24},{20,28},{24,16},{28,20},{1,9},{5... | collective-permute-start | bytes 116 | tf_op jit(solution)/shard_map/ppermute | solution.py:43
  20.2 4.5 %collective-permute-start.2 = (s32[1,9]{1,0:T(1,128)S(1)}, s32[1,9]{1,0:T(1,128)S(1)}, u32[]{:S(2)}, u32[]{:S(2)}) collective-permute-start(s32[1,9]{1,0:T(1,128)S(1)} %get-tuple-element.10), channel_id=1, source_target_pairs={{0,12},{4,8},{8,4},{12,0},{16,28},{20,24},{24,20},{28,16},{1,13},{... | collective-permute-start | bytes 116 | tf_op jit(solution)/shard_map/ppermute | solution.py:43
  26.2 12.8 %all-to-all-start = ((f32[8,9,128]{2,1,0:T(8,128)}), f32[8,9,128]{2,1,0:T(8,128)S(1)}, u32[]{:S(2)}, u32[]{:S(2)}) async-start(f32[8,9,128]{2,1,0:T(8,128)} %reshape.53), calls=%async_computation | async-start | bytes 131072 | tf_op jit(solution)/shard_map/all_to_all | solution.py:48
  39.6 4.1 %copy-start.2 = (s32[1,48]{1,0:T(1,128)S(1)}, s32[1,48]{1,0:T(1,128)}, u32[]{:S(2)}) copy-start(s32[1,48]{1,0:T(1,128)} %param.9) | copy-start | bytes 580
  39.6 26.7 %copy-start.1 = (s32[16,128]{1,0:T(8,128)S(1)}, s32[16,128]{1,0:T(8,128)}, u32[]{:S(2)}) copy-start(s32[16,128]{1,0:T(8,128)} %param.13) | copy-start | bytes 24580
  55.3 10.2 %all-to-all-start.1 = ((f32[8,9,128]{2,1,0:T(8,128)}), f32[8,9,128]{2,1,0:T(8,128)S(1)}, u32[]{:S(2)}, u32[]{:S(2)}) async-start(f32[8,9,128]{2,1,0:T(8,128)} %reshape.50), calls=%async_computation.1 | async-start | bytes 131072 | tf_op jit(solution)/shard_map/all_to_all | solution.py:56
